TPU v7x, 256 devices: a whole 4x4x8 slice. The times are simulated.
256 devices in a mesh: shift: 8 (over x, core), rows: 32 (over y, z).
Axes of the slice: x: 4, y: 4, z: 8, core: 2. Of those that a mesh axis runs over, the one named last changes fastest.
Arguments:
- neighbours: int32 [256, 8], P('rows'), may hold values from 0 to 255, as said below
- couplings: float32 [256, 8, 128, 128], P('rows'), may hold values from -0.01953125 to 0.01953125
- eigvectors: float32 [256, 128, 128], P('rows'), may hold values from -1 to 1, as said below
- eigvalues: float32 [256, 128], P('rows'), may hold values from -2.5 to 2.5
- start_block: float32 [32768, 128], P('rows'), may hold values from -240 to 240
Outputs:
- basis: float32 [32768, 128], P('rows')
- basis_image: float32 [32768, 128], P('rows')
- projected: float32 [128, 128], replicated
Inputs may be any that keep to these rules, and one draw needn't show every extreme that they name: Each block's 8 neighbours are distinct blocks other than itself, each within 8 blocks of it. `eigvectors`: each block's matrix has orthonormal columns up to rounding.
All inputs are finite; a program needn't handle non-finite values.
Results may differ from a plain program's by a relative error of at most 0.00025.
Values sent between devices are 32-bit elements; how exact they have to be, the bound alone decides.
A program may use at most 64 MiB of HBM per device.

v0:
```python
import jax
import jax.numpy as jnp
from jax import lax
from jax.sharding import PartitionSpec as P

SWEEPS = 3
radius = 1.0
damping = 0.8


def extended(block, sides, width):
    for axis, dim in sides:
        count = lax.axis_size(axis)
        forward = [(i, i + 1) for i in range(count - 1)]
        backward = [(target, source) for source, target in forward]
        low = lax.ppermute(
            lax.slice_in_dim(block, block.shape[dim] - width, None, axis=dim), axis, forward
        )
        high = lax.ppermute(lax.slice_in_dim(block, 0, width, axis=dim), axis, backward)
        block = jnp.concatenate([low, block, high], axis=dim)
    return block


def unrotate(vectors, field):
    return jnp.einsum("imn,imc->inc", vectors, field, precision=lax.Precision.HIGHEST)


def rotate(vectors, field):
    return jnp.einsum("inm,imc->inc", vectors, field, precision=lax.Precision.HIGHEST)


def shifted_inverse(vectors, values, field, real_part, imag_part):
    width = field.shape[-1] // 2
    spun = unrotate(vectors, field)
    offset = real_part - values
    denom = offset * offset + imag_part * imag_part
    scale_re = (offset / denom)[..., None]
    scale_im = (-imag_part / denom)[..., None]
    first = spun[..., :width]
    second = spun[..., width:]
    mixed = jnp.concatenate(
        [scale_re * first - scale_im * second, scale_re * second + scale_im * first], axis=-1
    )
    return rotate(vectors, mixed)


def diagonal_part(vectors, values, field):
    return rotate(vectors, values[..., None] * unrotate(vectors, field))


def coupled(near_blocks, couplings):
    return jnp.einsum("iknm,ikmc->inc", couplings, near_blocks, precision=lax.Precision.HIGHEST)


def product(left, right):
    return jnp.dot(left, right, precision=lax.Precision.HIGHEST)


def per_device(neighbours, couplings, eigvectors, eigvalues, start_block):
    blk_dev, blk = eigvalues.shape
    ncol = start_block.shape[1]
    rows_here = blk_dev * blk
    total = rows_here * lax.axis_size("rows")
    count = lax.axis_size("shift")
    angle = jnp.pi * (lax.axis_index("shift").astype(jnp.float32) + 0.5) / count
    real_part = radius * jnp.cos(angle)
    imag_part = radius * jnp.sin(angle)
    local_index = neighbours - (lax.axis_index("rows") * blk_dev - blk_dev)

    def operate_on(field, padded):
        blocks_all = padded.reshape(3 * blk_dev, blk, padded.shape[-1])
        near = blocks_all[local_index]
        return diagonal_part(eigvectors, eigvalues, field) + coupled(near, couplings)

    blocks_b = start_block.reshape(blk_dev, blk, ncol)
    rhs = jnp.concatenate([blocks_b, jnp.zeros_like(blocks_b)], axis=-1)
    iterate = damping * shifted_inverse(eigvectors, eigvalues, rhs, real_part, imag_part)
    for sweep in range(1, SWEEPS):
        first = iterate[..., :ncol]
        second = iterate[..., ncol:]
        shifted = jnp.concatenate(
            [real_part * first - imag_part * second, imag_part * first + real_part * second],
            axis=-1,
        )
        iterate_padded = extended(iterate.reshape(rows_here, 2 * ncol), (("rows", 0),), rows_here)
        resid = rhs - shifted + operate_on(iterate, iterate_padded)
        iterate = iterate + damping * shifted_inverse(
            eigvectors, eigvalues, resid, real_part, imag_part
        )
    contrib = real_part / count * iterate[..., :ncol] - imag_part / count * iterate[..., ncol:]
    contrib = contrib.reshape(rows_here, ncol)
    field = lax.psum(contrib, "shift")
    gram = lax.psum(product(field.T, field), "rows") / total
    factor = jnp.linalg.cholesky(gram)
    basis = jax.scipy.linalg.solve_triangular(factor, field.T, lower=True).T
    padded = extended(basis, (("rows", 0),), rows_here)
    image = operate_on(basis.reshape(blk_dev, blk, ncol), padded).reshape(rows_here, ncol)
    projected = lax.psum(product(basis.T, image), "rows") / total
    basis_image, projected = (image, projected)
    return (basis, basis_image, projected)


def solution(mesh):
    in_specs = (
        P("rows", None),
        P("rows", None, None, None),
        P("rows", None, None),
        P("rows", None),
        P("rows", None),
    )
    out_specs = (P("rows", None), P("rows", None), P())
    return jax.shard_map(
        per_device, mesh=mesh, in_specs=in_specs, out_specs=out_specs, check_vma=False
    )
```

profile of v0, /device:TPU:2, one launch (start us, length us, event | category | flops | bytes accessed | tf_op | source)
XLA Modules:
  0.0 556.1 jit_solution(6460307151305128019)
XLA Ops:
  12.9 4.8 collective-permute-start
  22.3 17.1 %collective-permute-done = f32[1024,256]{1,0:T(8,128)} collective-permute-done((f32[1024,256]{1,0:T(8,128)}, f32[1024,256]{1,0:T(8,128)}, u32[]{:S(2)}, u32[]{:S(2)}) %collective-permute-start) | collective-permute-done | bytes 1048608 | tf_op jit(solution)/shard_map/ppermute | solution.py:16
  39.4 5.1 collective-permute-done.1
  44.5 3.8 pad_maximum_fusion
  48.3 6.2 %gather_fusion = f32[64,128,256]{2,1,0:T(8,128)} fusion(f32[24,128,256]{2,1,0:T(8,128)} %bitcast.105, s32[1024]{0:T(1024)S(1)} %pad_clamp_fusion), kind=kCustom, calls=%fused_computation | custom fusion | bytes 16777472 | tf_op jit(solution)/shard_map/gather | solution.py:72
  54.5 17.7 %fusion.11 = f32[8,128,256]{1,2,0:T(8,128)S(1)} fusion(f32[8,256,128]{2,1,0:T(8,128)S(1)} %fusion.37, f32[8,8,128,256]{3,2,1,0:T(8,128)} %bitcast.108, f32[8,8,128,128]{3,2,1,0:T(8,128)} %param.6, f32[8,128,128]{1,2,0:T(8,128)S(1)} %copy.20, f32[8,128,128]{1,2,0:T(8,128)} %get-tuple-element.18, f32[8,128,128]{1,2,0:T(8,128)} %get-tuple-element.17), kind=kOutput, calls=%fused_computation.26 | convolution fusion | flops 3222274048 | bytes 16252928 | tf_op jit(solution)/shard_map/iknm,ikmc->inc/dot_general | solution.py:52
  75.8 4.0 collective-permute-start.2
  84.3 16.2 %collective-permute-done.2 = f32[1024,256]{1,0:T(8,128)} collective-permute-done((f32[1024,256]{1,0:T(8,128)}, f32[1024,256]{1,0:T(8,128)}, u32[]{:S(2)}, u32[]{:S(2)}) %collective-permute-start.2) | collective-permute-done | bytes 1048608 | tf_op jit(solution)/shard_map/ppermute | solution.py:16
  100.6 5.6 %collective-permute-done.3 = f32[1024,256]{1,0:T(8,128)} collective-permute-done((f32[1024,256]{1,0:T(8,128)}, f32[1024,256]{1,0:T(8,128)}, u32[]{:S(2)}, u32[]{:S(2)}) %collective-permute-start.3) | collective-permute-done | bytes 1048608 | tf_op jit(solution)/shard_map/ppermute | solution.py:19
  106.2 3.8 pad_maximum_fusion.1
  110.0 6.2 %gather_fusion.1 = f32[64,128,256]{2,1,0:T(8,128)} fusion(f32[24,128,256]{2,1,0:T(8,128)} %bitcast.106, s32[1024]{0:T(1024)S(1)} %pad_clamp_fusion), kind=kCustom, calls=%fused_computation.1 | custom fusion | bytes 16777472 | tf_op jit(solution)/shard_map/gather | solution.py:72
  116.2 17.3 %fusion.14 = f32[8,128,256]{1,2,0:T(8,128)S(1)} fusion(f32[8,256,128]{2,1,0:T(8,128)S(1)} %fusion.38, f32[8,8,128,256]{3,2,1,0:T(8,128)} %bitcast.107, f32[8,8,128,128]{3,2,1,0:T(8,128)} %param.6, f32[8,128,128]{1,2,0:T(8,128)S(1)} %copy.20, f32[8,128,128]{1,2,0:T(8,128)} %get-tuple-element.16, f32[8,128,128]{1,2,0:T(8,128)} %get-tuple-element.15), kind=kOutput, calls=%fused_computation.29 | convolution fusion | flops 3222274048 | bytes 16252928 | tf_op jit(solution)/shard_map/iknm,ikmc->inc/dot_general | solution.py:52
  137.0 65.0 %all-reduce.5.cloned.1.call-done = f32[1024,128]{1,0:T(8,128)} async-done(((f32[1024,128]{1,0:T(8,128)}), f32[1024,128]{1,0:T(8,128)}) %all-reduce.5.cloned.1.call-update) | async-done | bytes 524304 | tf_op jit(solution)/shard_map/psum | solution.py:92
  202.0 2.8 fusion.39
  205.1 143.7 %all-reduce.7.cloned.1.call-done = f32[128,128]{0,1:T(8,128)} async-done(((f32[128,128]{0,1:T(8,128)}), f32[128,128]{0,1:T(8,128)}) %all-reduce.7.cloned.1.call-update) | async-done | bytes 65552 | tf_op jit(solution)/shard_map/psum | solution.py:93
  350.5 11.7 %cholesky.16 = f32[128,128]{1,0:T(8,128)S(1)} custom-call(f32[128,128]{1,0:T(8,128)S(1)} %fusion.30), custom_call_target="Cholesky" | custom-call | tf_op jit(solution)/shard_map/jit(cholesky)/cholesky | solution.py:94
  363.6 9.8 %custom-call.7 = f32[1,128,128]{1,2,0:T(8,128)S(1)} custom-call(f32[1,128,128]{2,1,0:T(8,128)S(1)} %fusion.27), custom_call_target="InvertDiagBlocksLowerTriangular" | custom-call | tf_op jit(solution)/shard_map/jit(_solve_triangular)/triangular_solve | solution.py:95
  375.1 3.2 collective-permute-start.4
  380.5 4.7 collective-permute-done.4
  385.2 4.2 collective-permute-done.5
  390.6 1.9 copy.48
  392.5 2.8 gather_fusion.2
  395.3 8.1 %convolution_bitcast_fusion.4 = f32[8,128,128]{1,2,0:T(8,128)S(1)} fusion(f32[8,8,128,128]{3,2,1,0:T(8,128)} %bitcast.112, f32[8,8,128,128]{3,2,1,0:T(8,128)} %param.6), kind=kOutput, calls=%fused_computation.30 | convolution fusion | flops 1610612736 | bytes 8912896 | tf_op jit(solution)/shard_map/iknm,ikmc->inc/dot_general | solution.py:52
  407.2 140.5 %all-reduce.9.cloned.1.call-done = f32[128,128]{0,1:T(8,128)} async-done(((f32[128,128]{0,1:T(8,128)}), f32[128,128]{0,1:T(8,128)}) %all-reduce.9.cloned.1.call-update) | async-done | bytes 65552 | tf_op jit(solution)/shard_map/psum | solution.py:98
  (55 shorter events, 35.6 us)
Async XLA Ops:
  7.2 1.5 copy-start
  7.2 194.8 %all-reduce.5.cloned.1.call-start = ((), (), s32[]{:S(2)}) async-start(), calls=%async_computation | async-start | bytes 1048576 | tf_op jit(solution)/shard_map/psum | solution.py:92
  8.6 10.3 %copy-start.3 = (s32[8,8]{1,0:T(8,128)S(1)}, s32[8,8]{1,0:T(8,128)}, u32[]{:S(2)}) copy-start(s32[8,8]{1,0:T(8,128)} %param.5) | copy-start | bytes 772
  10.3 9.9 %copy-start.2 = (f32[8,128]{1,0:T(8,128)S(1)}, f32[8,128]{1,0:T(8,128)}, u32[]{:S(2)}) copy-start(f32[8,128]{1,0:T(8,128)} %param.8) | copy-start | bytes 12292
  12.9 26.5 %collective-permute-start = (f32[1024,256]{1,0:T(8,128)}, f32[1024,256]{1,0:T(8,128)}, u32[]{:S(2)}, u32[]{:S(2)}) collective-permute-start(f32[1024,256]{1,0:T(8,128)} %bitcast.3), channel_id=1, source_target_pairs={{0,1},{1,2},{2,3},{3,4},{4,5},{5,6},{6,7},{7,8},{8,9},{9,10},{10,1... | collective-permute-start | bytes 3145736 | tf_op jit(solution)/shard_map/ppermute | solution.py:16
  17.7 26.8 %collective-permute-start.1 = (f32[1024,256]{1,0:T(8,128)}, f32[1024,256]{1,0:T(8,128)}, u32[]{:S(2)}, u32[]{:S(2)}) collective-permute-start(f32[1024,256]{1,0:T(8,128)} %bitcast.3), channel_id=1, source_target_pairs={{1,0},{2,1},{3,2},{4,3},{5,4},{6,5},{7,6},{8,7},{9,8},{10,9},{11,1... | collective-permute-start | bytes 3145736 | tf_op jit(solution)/shard_map/ppermute | solution.py:19
  75.8 24.8 %collective-permute-start.2 = (f32[1024,256]{1,0:T(8,128)}, f32[1024,256]{1,0:T(8,128)}, u32[]{:S(2)}, u32[]{:S(2)}) collective-permute-start(f32[1024,256]{1,0:T(8,128)} %bitcast.11), channel_id=1, source_target_pairs={{0,1},{1,2},{2,3},{3,4},{4,5},{5,6},{6,7},{7,8},{8,9},{9,10},{10,1... | collective-permute-start | bytes 3145736 | tf_op jit(solution)/shard_map/ppermute | solution.py:16
  79.8 26.4 %collective-permute-start.3 = (f32[1024,256]{1,0:T(8,128)}, f32[1024,256]{1,0:T(8,128)}, u32[]{:S(2)}, u32[]{:S(2)}) collective-permute-start(f32[1024,256]{1,0:T(8,128)} %bitcast.11), channel_id=1, source_target_pairs={{1,0},{2,1},{3,2},{4,3},{5,4},{6,5},{7,6},{8,7},{9,8},{10,9},{11,1... | collective-permute-start | bytes 3145736 | tf_op jit(solution)/shard_map/ppermute | solution.py:19
  136.9 211.8 %all-reduce.7.cloned.1.call-start = ((), (), s32[]{:S(2)}) async-start(), calls=%async_computation.1 | async-start | bytes 131072 | tf_op jit(solution)/shard_map/psum | solution.py:93
  204.8 342.9 %all-reduce.9.cloned.1.call-start = ((), (), s32[]{:S(2)}) async-start(), calls=%async_computation.2 | async-start | bytes 131072 | tf_op jit(solution)/shard_map/psum | solution.py:98
  375.1 10.1 %collective-permute-start.4 = (f32[1024,128]{0,1:T(8,128)S(1)}, f32[1024,128]{0,1:T(8,128)S(1)}, u32[]{:S(2)}, u32[]{:S(2)}) collective-permute-start(f32[1024,128]{0,1:T(8,128)S(1)} %bitcast.113), channel_id=1, source_target_pairs={{0,1},{1,2},{2,3},{3,4},{4,5},{5,6},{6,7},{7,8},{8,9},{9,10},{10,1... | collective-permute-start | bytes 1572872 | tf_op jit(solution)/shard_map/ppermute | solution.py:16
  378.3 11.1 %collective-permute-start.5 = (f32[1024,128]{0,1:T(8,128)S(1)}, f32[1024,128]{0,1:T(8,128)S(1)}, u32[]{:S(2)}, u32[]{:S(2)}) collective-permute-start(f32[1024,128]{0,1:T(8,128)S(1)} %bitcast.114), channel_id=1, source_target_pairs={{1,0},{2,1},{3,2},{4,3},{5,4},{6,5},{7,6},{8,7},{9,8},{10,9},{11,1... | collective-permute-start | bytes 1572872 | tf_op jit(solution)/shard_map/ppermute | solution.py:19
  404.6 144.7 %copy-start.1 = (f32[8,128,128]{1,2,0:T(8,128)}, f32[8,128,128]{1,2,0:T(8,128)S(1)}, u32[]{:S(2)}) copy-start(f32[8,128,128]{1,2,0:T(8,128)S(1)} %convolution_add_fusion) | copy-start | bytes 1572868
Sparse Core Ops, SparseCore 0:
  137.1 64.8 all-reduce.4
  206.0 142.7 all-reduce.6
  406.4 141.3 all-reduce.8
where the time goes:
time: 562 us; the launch traced here: 556 us
  waiting for transfers between devices  402 us (72%)
  matrix products  61.7 us (11%)
  other arithmetic  37.6 us (7%)
  local copies, waits for them, and re-layouts  23.8 us (4%)
  starting transfers between devices  16.5 us (3%)
  between operations  14.5 us (3%)
    psum x1, waiting for transfers between devices, per_device(): gram = lax.psum(product(field.T, field), 'rows') / total  144 us
    psum x1, waiting for transfers between devices, per_device(): projected = lax.psum(product(basis.T, image), 'rows') / total  140 us
    psum x1, waiting for transfers between devices, per_device(): field = lax.psum(contrib, 'shift')  65 us
    dot_general x3, matrix products, coupled(): jnp.einsum('iknm,ikmc->inc', couplings, near_blocks, precision=lax.Precis...  43.1 us
    ppermute x3, waiting for transfers between devices, extended(): lax.ppermute(lax.slice_in_dim(block, block.shape[dim] - width, None, axis...  38 us
    gather x3, local copies, waits for them, and re-layouts, operate_on(): near = blocks_all[local_index]  15.2 us
    ppermute x3, waiting for transfers between devices, extended(): lax.ppermute(lax.slice_in_dim(block, 0, width, axis=dim), axis, backward)  14.9 us
    another operation x3, other arithmetic, per_device(): factor = jnp.linalg.cholesky(gram)  12.4 us
  transfers between devices with their start and end apart: 9, of which 9 were waited for; matrix products, arithmetic and copies ran while one was open for 1% of the time, Pallas kernels for 0%

commit v1 on v0

--- a/solution.py
+++ b/solution.py
@@ -89,7 +89,9 @@
         )
     contrib = real_part / count * iterate[..., :ncol] - imag_part / count * iterate[..., ncol:]
     contrib = contrib.reshape(rows_here, ncol)
-    field = lax.psum(contrib, "shift")
+    field = contrib
+    for hop in (1, 2, 4):
+        field = field + lax.ppermute(field, "shift", [(dev, dev ^ hop) for dev in range(8)])
     gram = lax.psum(product(field.T, field), "rows") / total
     factor = jnp.linalg.cholesky(gram)
     basis = jax.scipy.linalg.solve_triangular(factor, field.T, lower=True).T

time: 562 us -> 523 us (0.931)
  waiting for transfers between devices: 402 us -> 364 us
    psum x1 -> x0, waiting for transfers between devices: 65 us -> none  [per_device(): field = lax.psum(contrib, 'shift')]
    ppermute x0 -> x3, waiting for transfers between devices: none -> 27.8 us  [per_device(): lax.ppermute(field, 'shift', [(dev, dev ^ hop) for dev in range(8)])]
  transfers between devices with their start and end apart: 9 -> 11, of which waited for: 9 -> 11; matrix products, arithmetic and copies ran while one was open for 1% -> 2% of each run, Pallas kernels for 0% -> 0%
where the time goes in v1:
time: 523 us; the launch traced here: 518 us
  waiting for transfers between devices  364 us (70%)
  matrix products  59.4 us (11%)
  other arithmetic  37.8 us (7%)
  local copies, waits for them, and re-layouts  23 us (4%)
  starting transfers between devices  19.3 us (4%)
  between operations  14.8 us (3%)
    psum x1, waiting for transfers between devices, per_device(): gram = lax.psum(product(field.T, field), 'rows') / total  142 us
    psum x1, waiting for transfers between devices, per_device(): projected = lax.psum(product(basis.T, image), 'rows') / total  141 us
    dot_general x3, matrix products, coupled(): jnp.einsum('iknm,ikmc->inc', couplings, near_blocks, precision=lax.Precis...  43.1 us
    ppermute x3, waiting for transfers between devices, extended(): lax.ppermute(lax.slice_in_dim(block, block.shape[dim] - width, None, axis...  38.1 us
    ppermute x3, waiting for transfers between devices, per_device(): lax.ppermute(field, 'shift', [(dev, dev ^ hop) for dev in range(8)])  27.8 us
    gather x3, local copies, waits for them, and re-layouts, operate_on(): near = blocks_all[local_index]  15.2 us
    ppermute x3, waiting for transfers between devices, extended(): lax.ppermute(lax.slice_in_dim(block, 0, width, axis=dim), axis, backward)  14.8 us
    another operation x3, other arithmetic, per_device(): factor = jnp.linalg.cholesky(gram)  12.4 us
  transfers between devices with their start and end apart: 11, of which 11 were waited for; matrix products, arithmetic and copies ran while one was open for 2% of the time, Pallas kernels for 0%

profile of v1, /device:TPU:2, one launch (start us, length us, event | category | flops | bytes accessed | tf_op | source)
XLA Modules:
  0.0 518.0 jit_solution(1652321847701035332)
XLA Ops:
  12.9 4.8 collective-permute-start
  22.3 17.1 %collective-permute-done = f32[1024,256]{1,0:T(8,128)} collective-permute-done((f32[1024,256]{1,0:T(8,128)}, f32[1024,256]{1,0:T(8,128)}, u32[]{:S(2)}, u32[]{:S(2)}) %collective-permute-start) | collective-permute-done | bytes 1048608 | tf_op jit(solution)/shard_map/ppermute | solution.py:16
  39.4 5.1 collective-permute-done.1
  44.5 3.8 pad_maximum_fusion
  48.2 6.2 %gather_fusion = f32[64,128,256]{2,1,0:T(8,128)} fusion(f32[24,128,256]{2,1,0:T(8,128)} %bitcast.106, s32[1024]{0:T(1024)S(1)} %pad_clamp_fusion), kind=kCustom, calls=%fused_computation | custom fusion | bytes 16777472 | tf_op jit(solution)/shard_map/gather | solution.py:72
  54.4 17.7 %fusion.11 = f32[8,128,256]{1,2,0:T(8,128)S(1)} fusion(f32[8,256,128]{2,1,0:T(8,128)S(1)} %fusion.37, f32[8,8,128,256]{3,2,1,0:T(8,128)} %bitcast.109, f32[8,8,128,128]{3,2,1,0:T(8,128)} %param.6, f32[8,128,128]{1,2,0:T(8,128)S(1)} %copy.20, f32[8,128,128]{1,2,0:T(8,128)} %get-tuple-element.18, f32[8,128,128]{1,2,0:T(8,128)} %get-tuple-element.17), kind=kOutput, calls=%fused_computation.26 | convolution fusion | flops 3222274048 | bytes 16252928 | tf_op jit(solution)/shard_map/iknm,ikmc->inc/dot_general | solution.py:52
  75.8 4.0 collective-permute-start.2
  84.3 16.3 %collective-permute-done.2 = f32[1024,256]{1,0:T(8,128)} collective-permute-done((f32[1024,256]{1,0:T(8,128)}, f32[1024,256]{1,0:T(8,128)}, u32[]{:S(2)}, u32[]{:S(2)}) %collective-permute-start.2) | collective-permute-done | bytes 1048608 | tf_op jit(solution)/shard_map/ppermute | solution.py:16
  100.6 5.6 %collective-permute-done.3 = f32[1024,256]{1,0:T(8,128)} collective-permute-done((f32[1024,256]{1,0:T(8,128)}, f32[1024,256]{1,0:T(8,128)}, u32[]{:S(2)}, u32[]{:S(2)}) %collective-permute-start.3) | collective-permute-done | bytes 1048608 | tf_op jit(solution)/shard_map/ppermute | solution.py:19
  106.2 3.8 pad_maximum_fusion.1
  109.9 6.2 %gather_fusion.1 = f32[64,128,256]{2,1,0:T(8,128)} fusion(f32[24,128,256]{2,1,0:T(8,128)} %bitcast.107, s32[1024]{0:T(1024)S(1)} %pad_clamp_fusion), kind=kCustom, calls=%fused_computation.1 | custom fusion | bytes 16777472 | tf_op jit(solution)/shard_map/gather | solution.py:72
  116.1 17.3 %fusion.14 = f32[8,128,256]{1,2,0:T(8,128)S(1)} fusion(f32[8,256,128]{2,1,0:T(8,128)S(1)} %fusion.38, f32[8,8,128,256]{3,2,1,0:T(8,128)} %bitcast.108, f32[8,8,128,128]{3,2,1,0:T(8,128)} %param.6, f32[8,128,128]{1,2,0:T(8,128)S(1)} %copy.20, f32[8,128,128]{1,2,0:T(8,128)} %get-tuple-element.16, f32[8,128,128]{1,2,0:T(8,128)} %get-tuple-element.15), kind=kOutput, calls=%fused_computation.29 | convolution fusion | flops 3222274048 | bytes 16252928 | tf_op jit(solution)/shard_map/iknm,ikmc->inc/dot_general | solution.py:52
  138.8 13.4 %collective-permute-done.5 = f32[1024,128]{1,0:T(8,128)S(1)} collective-permute-done((f32[1024,128]{1,0:T(8,128)S(1)}, f32[1024,128]{1,0:T(8,128)S(1)}, u32[]{:S(2)}, u32[]{:S(2)}) %collective-permute-start.5) | collective-permute-done | bytes 524320 | tf_op jit(solution)/shard_map/ppermute | solution.py:94
  152.3 2.4 collective-permute-start.6
  154.7 12.5 %collective-permute-done.6 = f32[1024,128]{1,0:T(8,128)S(1)} collective-permute-done((f32[1024,128]{1,0:T(8,128)S(1)}, f32[1024,128]{1,0:T(8,128)S(1)}, u32[]{:S(2)}, u32[]{:S(2)}) %collective-permute-start.6) | collective-permute-done | bytes 524320 | tf_op jit(solution)/shard_map/ppermute | solution.py:94
  168.9 142.4 %all-reduce.4.cloned.1.call-done = f32[128,128]{0,1:T(8,128)} async-done(((f32[128,128]{0,1:T(8,128)}), f32[128,128]{0,1:T(8,128)}) %all-reduce.4.cloned.1.call-update) | async-done | bytes 65552 | tf_op jit(solution)/shard_map/psum | solution.py:95
  313.2 11.7 %cholesky.16 = f32[128,128]{1,0:T(8,128)S(1)} custom-call(f32[128,128]{1,0:T(8,128)S(1)} %fusion.30), custom_call_target="Cholesky" | custom-call | tf_op jit(solution)/shard_map/jit(cholesky)/cholesky | solution.py:96
  326.2 9.8 %custom-call.7 = f32[1,128,128]{1,2,0:T(8,128)S(1)} custom-call(f32[1,128,128]{2,1,0:T(8,128)S(1)} %fusion.27), custom_call_target="InvertDiagBlocksLowerTriangular" | custom-call | tf_op jit(solution)/shard_map/jit(_solve_triangular)/triangular_solve | solution.py:97
  336.7 3.2 collective-permute-start.7
  342.1 4.7 collective-permute-done.7
  346.8 4.2 collective-permute-done.8
  354.1 2.8 gather_fusion.2
  356.9 8.1 %convolution_bitcast_fusion.4 = f32[8,128,128]{1,2,0:T(8,128)S(1)} fusion(f32[8,8,128,128]{3,2,1,0:T(8,128)} %bitcast.113, f32[8,8,128,128]{3,2,1,0:T(8,128)} %param.6), kind=kOutput, calls=%fused_computation.30 | convolution fusion | flops 1610612736 | bytes 8912896 | tf_op jit(solution)/shard_map/iknm,ikmc->inc/dot_general | solution.py:52
  368.8 140.5 %all-reduce.6.cloned.1.call-done = f32[128,128]{0,1:T(8,128)} async-done(((f32[128,128]{0,1:T(8,128)}), f32[128,128]{0,1:T(8,128)}) %all-reduce.6.cloned.1.call-update) | async-done | bytes 65552 | tf_op jit(solution)/shard_map/psum | solution.py:100
  (61 shorter events, 39.8 us)
Async XLA Ops:
  7.2 1.5 copy-start
  7.2 304.2 %all-reduce.4.cloned.1.call-start = ((), (), s32[]{:S(2)}) async-start(), calls=%async_computation | async-start | bytes 131072 | tf_op jit(solution)/shard_map/psum | solution.py:95
  8.6 10.3 %copy-start.3 = (s32[8,8]{1,0:T(8,128)S(1)}, s32[8,8]{1,0:T(8,128)}, u32[]{:S(2)}) copy-start(s32[8,8]{1,0:T(8,128)} %param.5) | copy-start | bytes 772
  10.3 9.8 %copy-start.2 = (f32[8,128]{1,0:T(8,128)S(1)}, f32[8,128]{1,0:T(8,128)}, u32[]{:S(2)}) copy-start(f32[8,128]{1,0:T(8,128)} %param.8) | copy-start | bytes 12292
  12.9 26.5 %collective-permute-start = (f32[1024,256]{1,0:T(8,128)}, f32[1024,256]{1,0:T(8,128)}, u32[]{:S(2)}, u32[]{:S(2)}) collective-permute-start(f32[1024,256]{1,0:T(8,128)} %bitcast.3), channel_id=1, source_target_pairs={{0,1},{1,2},{2,3},{3,4},{4,5},{5,6},{6,7},{7,8},{8,9},{9,10},{10,1... | collective-permute-start | bytes 3145736 | tf_op jit(solution)/shard_map/ppermute | solution.py:16
  17.7 26.8 %collective-permute-start.1 = (f32[1024,256]{1,0:T(8,128)}, f32[1024,256]{1,0:T(8,128)}, u32[]{:S(2)}, u32[]{:S(2)}) collective-permute-start(f32[1024,256]{1,0:T(8,128)} %bitcast.3), channel_id=1, source_target_pairs={{1,0},{2,1},{3,2},{4,3},{5,4},{6,5},{7,6},{8,7},{9,8},{10,9},{11,1... | collective-permute-start | bytes 3145736 | tf_op jit(solution)/shard_map/ppermute | solution.py:19
  75.8 24.8 %collective-permute-start.2 = (f32[1024,256]{1,0:T(8,128)}, f32[1024,256]{1,0:T(8,128)}, u32[]{:S(2)}, u32[]{:S(2)}) collective-permute-start(f32[1024,256]{1,0:T(8,128)} %bitcast.11), channel_id=1, source_target_pairs={{0,1},{1,2},{2,3},{3,4},{4,5},{5,6},{6,7},{7,8},{8,9},{9,10},{10,1... | collective-permute-start | bytes 3145736 | tf_op jit(solution)/shard_map/ppermute | solution.py:16
  79.8 26.4 %collective-permute-start.3 = (f32[1024,256]{1,0:T(8,128)}, f32[1024,256]{1,0:T(8,128)}, u32[]{:S(2)}, u32[]{:S(2)}) collective-permute-start(f32[1024,256]{1,0:T(8,128)} %bitcast.11), channel_id=1, source_target_pairs={{1,0},{2,1},{3,2},{4,3},{5,4},{6,5},{7,6},{8,7},{9,8},{10,9},{11,1... | collective-permute-start | bytes 3145736 | tf_op jit(solution)/shard_map/ppermute | solution.py:19
  136.1 2.0 collective-permute-start.4
  138.2 14.1 %collective-permute-start.5 = (f32[1024,128]{1,0:T(8,128)S(1)}, f32[1024,128]{1,0:T(8,128)S(1)}, u32[]{:S(2)}, u32[]{:S(2)}) collective-permute-start(f32[1024,128]{1,0:T(8,128)S(1)} %bitcast_add_fusion.1), channel_id=1, source_target_pairs={{0,64},{32,96},{64,0},{96,32},{128,192},{160,224},{192,128},{224,1... | collective-permute-start | bytes 1572872 | tf_op jit(solution)/shard_map/ppermute | solution.py:94
  152.3 14.9 %collective-permute-start.6 = (f32[1024,128]{1,0:T(8,128)S(1)}, f32[1024,128]{1,0:T(8,128)S(1)}, u32[]{:S(2)}, u32[]{:S(2)}) collective-permute-start(f32[1024,128]{1,0:T(8,128)S(1)} %add.109), channel_id=1, source_target_pairs={{0,128},{32,160},{64,192},{96,224},{128,0},{160,32},{192,64},{224,... | collective-permute-start | bytes 1572872 | tf_op jit(solution)/shard_map/ppermute | solution.py:94
  168.9 340.4 %all-reduce.6.cloned.1.call-start = ((), (), s32[]{:S(2)}) async-start(), calls=%async_computation.1 | async-start | bytes 131072 | tf_op jit(solution)/shard_map/psum | solution.py:100
  336.7 10.1 %collective-permute-start.7 = (f32[1024,128]{0,1:T(8,128)S(1)}, f32[1024,128]{0,1:T(8,128)S(1)}, u32[]{:S(2)}, u32[]{:S(2)}) collective-permute-start(f32[1024,128]{0,1:T(8,128)S(1)} %bitcast.114), channel_id=1, source_target_pairs={{0,1},{1,2},{2,3},{3,4},{4,5},{5,6},{6,7},{7,8},{8,9},{9,10},{10,1... | collective-permute-start | bytes 1572872 | tf_op jit(solution)/shard_map/ppermute | solution.py:16
  339.9 11.1 %collective-permute-start.8 = (f32[1024,128]{0,1:T(8,128)S(1)}, f32[1024,128]{0,1:T(8,128)S(1)}, u32[]{:S(2)}, u32[]{:S(2)}) collective-permute-start(f32[1024,128]{0,1:T(8,128)S(1)} %bitcast.115), channel_id=1, source_target_pairs={{1,0},{2,1},{3,2},{4,3},{5,4},{6,5},{7,6},{8,7},{9,8},{10,9},{11,1... | collective-permute-start | bytes 1572872 | tf_op jit(solution)/shard_map/ppermute | solution.py:19
  366.2 144.7 %copy-start.1 = (f32[8,128,128]{1,2,0:T(8,128)}, f32[8,128,128]{1,2,0:T(8,128)S(1)}, u32[]{:S(2)}) copy-start(f32[8,128,128]{1,2,0:T(8,128)S(1)} %convolution_add_fusion) | copy-start | bytes 1572868
Sparse Core Ops, SparseCore 0:
  169.0 142.3 all-reduce.3
  368.0 141.3 all-reduce.5
